TPU v7x, 256 devices: a whole 4x4x8 slice. The times are simulated.
256 devices in a mesh: row: 16 (over x, y_lo, core), col: 8 (over z), slab: 2 (over y_hi).
Axes of the slice: x: 4, y: 4 (y_hi: 2, y_lo: 2; y = y_hi * 2 + y_lo), z: 8, core: 2. Of those that a mesh axis runs over, the one named last changes fastest.
Arguments:
- fields: bfloat16 [2, 16384, 1024], P(None, ('row', 'col', 'slab')), may hold values from -0.8984375 to 0.8984375
Outputs:
- gram: float32 [2, 16384, 16384], P(None, ('row', 'slab'), 'col')
All inputs are finite; a program needn't handle non-finite values.
Results may differ from a plain program's by a relative error of at most 0.01.
Values may be sent and summed in bfloat16 or wider, within the bound.
A program may use at most 64 MiB of HBM per device.

v0:
```python
import jax
import jax.numpy as jnp
from jax import lax
from jax.sharding import PartitionSpec as P


def pair_terms(left_real, left_imag, piece):
    right_real = jnp.concatenate([piece[0], piece[1]], axis=1)
    right_imag = jnp.concatenate([piece[1], piece[0]], axis=1)
    dims = (((1,), (1,)), ((), ()))
    real = lax.dot_general(left_real, right_real, dims, preferred_element_type=jnp.float32)
    imag = lax.dot_general(left_imag, right_imag, dims, preferred_element_type=jnp.float32)
    return jnp.stack([real, imag])


def body(fields):
    local = lax.all_to_all(fields, "slab", split_axis=2, concat_axis=1, tiled=True)
    row_block = lax.all_gather(local, "col", axis=1, tiled=True)
    left_real = jnp.concatenate([row_block[0], row_block[1]], axis=1)
    left_imag = jnp.concatenate([row_block[0], -row_block[1]], axis=1)
    column_set = lax.all_gather(local, "row", axis=1, tiled=True)
    terms = pair_terms(left_real, left_imag, column_set)
    gram = lax.psum_scatter(
        terms.astype(jnp.bfloat16), "slab", scatter_dimension=1, tiled=True
    ).astype(jnp.float32)
    return gram


def solution(mesh):
    placed = (P(None, ("row", "col", "slab"), None),)
    return jax.shard_map(
        body, mesh=mesh, in_specs=placed, out_specs=P(None, ("row", "slab"), "col"), check_vma=False
    )
```

profile of v0, /device:TPU:1, one launch (start us, length us, event | category | flops | bytes accessed | tf_op | source)
XLA Modules:
  0.0 242.6 jit_solution(3190334933049715580)
XLA Ops:
  6.5 0.0 all-gather.3.cloned.1.call-start
  6.5 1.3 copy.3
  7.8 0.4 reshape
  8.2 10.3 %all_to_all.18 = bf16[2,2,32768]{2,1,0:T(2,128)(2,1)S(1)} all-to-all(bf16[2,2,32768]{2,1,0:T(2,128)(2,1)S(1)} %reshape), channel_id=1, replica_groups=mesh['row'=16,'col'=8,'slab'=2] {'slab'}, dimensions={0} | all-to-all | bytes 524288 | tf_op jit(solution)/shard_map/all_to_all | solution.py:17
  18.6 0.3 reshape.1
  18.9 1.0 copy.5
  19.9 0.0 all-gather.3.cloned.1.call-update
  19.9 0.0 all-gather.5.cloned.1.call-start
  20.0 0.7 all-gather.5.cloned.1.call-update
  20.7 0.0 reduce-scatter.2.cloned.1.call-start
  20.7 38.7 %all-gather.3.cloned.1.call-done = bf16[2,1024,512]{2,1,0:T(8,128)(2,1)} async-done(((bf16[2,128,512]{2,1,0:T(8,128)(2,1)}), bf16[2,1024,512]{2,1,0:T(8,128)(2,1)}) %all-gather.3.cloned.1.call-update) | async-done | bytes 2097168 | tf_op jit(solution)/shard_map/all_gather | solution.py:18
  59.4 1.3 fusion.16
  60.7 2.6 %slice_bitcast_fusion.2 = (bf16[1024,512]{1,0:T(8,128)(2,1)}, bf16[1024,512]{1,0:T(8,128)(2,1)S(1)}) fusion(bf16[2,1024,512]{2,1,0:T(8,128)(2,1)} %all-gather.3.cloned.1.call-done), kind=kLoop, calls=%fused_computation.17 | loop fusion | bytes 4194304 | tf_op jit(solution)/shard_map/squeeze | solution.py:19
  63.3 40.4 %all-gather.5.cloned.1.call-done = bf16[2,2048,512]{2,1,0:T(8,128)(2,1)} async-done(((bf16[2,128,512]{2,1,0:T(8,128)(2,1)}), bf16[2,2048,512]{2,1,0:T(8,128)(2,1)}) %all-gather.5.cloned.1.call-update) | async-done | bytes 4194320 | tf_op jit(solution)/shard_map/all_gather | solution.py:21
  103.8 0.0 copy-start
  103.8 2.6 %slice_bitcast_fusion = (bf16[2048,512]{1,0:T(8,128)(2,1)S(1)}, bf16[2048,512]{1,0:T(8,128)(2,1)S(1)}) fusion(bf16[2,2048,512]{2,1,0:T(8,128)(2,1)} %all-gather.5.cloned.1.call-done), kind=kLoop, calls=%fused_computation.13 | loop fusion | bytes 8388608 | tf_op jit(solution)/shard_map/squeeze | solution.py:8
  106.3 0.0 copy-done
  106.3 4.8 %convert_bitcast_fusion.1 = bf16[1,1024,2048]{2,1,0:T(8,128)(2,1)S(1)} fusion(bf16[2048,512]{1,0:T(8,128)(2,1)S(1)} %get-tuple-element.5, bf16[2048,512]{1,0:T(8,128)(2,1)S(1)} %get-tuple-element.6, bf16[1024,512]{1,0:T(8,128)(2,1)S(1)} %get-tuple-element.8, bf16[1024,512]{1,0:T(8,128)(2,1)S(1)} %copy-done), kind=kOutput, calls=%fused_computation.10 | convolution fusion | flops 4309647360 | bytes 10485760 | tf_op jit(solution)/shard_map/dot_general | solution.py:11
  111.1 6.1 %convert_bitcast_fusion = bf16[1,1024,2048]{2,1,0:T(8,128)(2,1)} fusion(bf16[2048,512]{1,0:T(8,128)(2,1)S(1)} %get-tuple-element.6, bf16[2048,512]{1,0:T(8,128)(2,1)S(1)} %get-tuple-element.5, bf16[1024,512]{1,0:T(8,128)(2,1)S(1)} %get-tuple-element.8, bf16[1024,512]{1,0:T(8,128)(2,1)S(1)} %fusion.16), kind=kOutput, calls=%fused_computation.9 | convolution fusion | flops 4309647360 | bytes 10485760 | tf_op jit(solution)/shard_map/dot_general | solution.py:12
  117.3 6.3 %pad_maximum_fusion = bf16[2,1024,2048]{2,1,0:T(8,128)(2,1)} fusion(bf16[1,1024,2048]{2,1,0:T(8,128)(2,1)} %convert_bitcast_fusion, bf16[1,1024,2048]{2,1,0:T(8,128)(2,1)S(1)} %convert_bitcast_fusion.1), kind=kLoop, calls=%fused_computation | loop fusion | flops 4194304 | bytes 16777216 | tf_op jit(solution)/shard_map/stack | solution.py:13
  123.6 0.0 reduce-scatter.2.cloned.1.call-update
  123.6 105.7 %reduce-scatter.2.cloned.1.call-done = bf16[2,512,2048]{2,1,0:T(8,128)(2,1)} async-done(((bf16[2,1024,2048]{2,1,0:T(8,128)(2,1)}), bf16[2,512,2048]{2,1,0:T(8,128)(2,1)}) %reduce-scatter.2.cloned.1.call-update) | async-done | bytes 4194320 | tf_op jit(solution)/shard_map/reduce_scatter | solution.py:23
  229.4 6.7 %convert_element_type.4 = f32[2,512,2048]{2,1,0:T(8,128)} convert(bf16[2,512,2048]{2,1,0:T(8,128)(2,1)} %reduce-scatter.2.cloned.1.call-done) | non-fusion elementwise | flops 2097152 | bytes 12582912 | tf_op jit(solution)/shard_map/convert_element_type | solution.py:25
Async XLA Ops:
  6.5 52.9 %all-gather.3.cloned.1.call-start = ((), (), s32[]{:S(2)}) async-start(), calls=%async_computation.2 | async-start | bytes 2359296 | tf_op jit(solution)/shard_map/all_gather | solution.py:18
  19.9 83.8 %all-gather.5.cloned.1.call-start = ((), (), s32[]{:S(2)}) async-start(), calls=%async_computation.3 | async-start | bytes 4456448 | tf_op jit(solution)/shard_map/all_gather | solution.py:21
  20.7 208.7 %reduce-scatter.2.cloned.1.call-start = ((), (), s32[]{:S(2)}) async-start(), calls=%async_computation.4 | async-start | bytes 12582912 | tf_op jit(solution)/shard_map/reduce_scatter | solution.py:23
  103.8 2.6 %copy-start = (bf16[1024,512]{1,0:T(8,128)(2,1)S(1)}, bf16[1024,512]{1,0:T(8,128)(2,1)}, u32[]{:S(2)}) copy-start(bf16[1024,512]{1,0:T(8,128)(2,1)} %get-tuple-element.7) | copy-start | bytes 3145732
Sparse Core Ops, SparseCore 0:
  20.1 39.2 all-gather.2
  61.2 42.4 all-gather.4
  123.8 105.5 reduce-scatter.1
where the time goes:
time: 243 us
  waiting for transfers between devices  186 us (77%)
  other arithmetic  14.3 us (6%)
  between operations  13.2 us (5%)
  matrix products  10.9 us (4%)
  blocking collectives  10.3 us (4%)
  local copies, waits for them, and re-layouts  8.25 us (3%)
    reduce_scatter x1, waiting for transfers between devices, body(): lax.psum_scatter(terms.astype(jnp.bfloat16), 'slab', scatter_dimension=1,...  106 us
    all_gather x1, waiting for transfers between devices, body(): column_set = lax.all_gather(local, 'row', axis=1, tiled=True)  40.4 us
    all_gather x1, waiting for transfers between devices, body(): row_block = lax.all_gather(local, 'col', axis=1, tiled=True)  38.7 us
    all_to_all x1, blocking collectives, body(): lax.all_to_all(fields, 'slab', split_axis=2, concat_axis=1, tiled=True)  10.3 us
    convert_element_type x1, other arithmetic, body(): gram = lax.psum_scatter(terms.astype(jnp.bfloat16), 'slab', scatter_dimen...  6.65 us
    another operation x1, other arithmetic, pair_terms(): return jnp.stack([real, imag])  6.35 us
    dot_general x1, matrix products, pair_terms(): lax.dot_general(left_imag, right_imag, dims, preferred_element_type=jnp.f...  6.13 us
  transfers between devices with their start and end apart: 3, of which 3 were waited for; matrix products, arithmetic and copies ran while one was open for 2% of the time, Pallas kernels for 0%

commit v1 on v0

--- a/solution.py
+++ b/solution.py
@@ -15,7 +15,22 @@
 
 def body(fields):
     local = lax.all_to_all(fields, "slab", split_axis=2, concat_axis=1, tiled=True)
-    row_block = lax.all_gather(local, "col", axis=1, tiled=True)
+    ways, here, step = (lax.axis_size("col"), lax.axis_index("col"), local.shape[1])
+    dims_2 = [n * ways if d == 1 else n for d, n in enumerate(local.shape)]
+    row_block = lax.dynamic_update_slice_in_dim(
+        jnp.zeros(dims_2, local.dtype), local, here * step, axis=1
+    )
+    going_up = going_down = local
+    for far in range(1, ways // 2 + 1):
+        going_up = lax.ppermute(going_up, "col", [(d, (d + 1) % ways) for d in range(ways)])
+        row_block = lax.dynamic_update_slice_in_dim(
+            row_block, going_up, (here - far) % ways * step, axis=1
+        )
+        if 2 * far < ways:
+            going_down = lax.ppermute(going_down, "col", [(d, (d - 1) % ways) for d in range(ways)])
+            row_block = lax.dynamic_update_slice_in_dim(
+                row_block, going_down, (here + far) % ways * step, axis=1
+            )
     left_real = jnp.concatenate([row_block[0], row_block[1]], axis=1)
     left_imag = jnp.concatenate([row_block[0], -row_block[1]], axis=1)
     column_set = lax.all_gather(local, "row", axis=1, tiled=True)

time: 243 us -> 202 us (0.83)
  waiting for transfers between devices: 186 us -> 135 us
  starting transfers between devices: 0.08 us -> 11.2 us
    all_gather x1 -> x0, waiting for transfers between devices: 38.7 us -> none  [body(): row_block = lax.all_gather(local, 'col', axis=1, tiled=True)]
    all_gather x1, waiting for transfers between devices: 40.4 us -> 10.6 us  [body(): column_set = lax.all_gather(local, 'row', axis=1, tiled=True)]
    ppermute x0 -> x7, waiting for transfers between devices: none -> 18.9 us  [the longest x4 18.8 us: body(): lax.ppermute(going_up, 'col', [(d, (d + 1) % ways) for d in range(ways)])]
    ppermute x0 -> x7, starting transfers between devices: none -> 11.2 us  [the longest x3 9.45 us: body(): lax.ppermute(going_down, 'col', [(d, (d - 1) % ways) for d in range(ways)])]
  transfers between devices with their start and end apart: 3 -> 9, of which waited for: 3 -> 6; matrix products, arithmetic and copies ran while one was open for 2% -> 1% of each run, Pallas kernels for 0% -> 0%
where the time goes in v1:
time: 202 us; the launch traced here: 201 us
  waiting for transfers between devices  135 us (67%)
  between operations  13.5 us (7%)
  other arithmetic  13.1 us (6%)
  starting transfers between devices  11.2 us (6%)
  matrix products  10.9 us (5%)
  blocking collectives  10.3 us (5%)
  local copies, waits for them, and re-layouts  7.07 us (4%)
    reduce_scatter x1, waiting for transfers between devices, body(): lax.psum_scatter(terms.astype(jnp.bfloat16), 'slab', scatter_dimension=1,...  106 us
    ppermute x4, waiting for transfers between devices, body(): lax.ppermute(going_up, 'col', [(d, (d + 1) % ways) for d in range(ways)])  18.8 us
    all_gather x1, waiting for transfers between devices, body(): column_set = lax.all_gather(local, 'row', axis=1, tiled=True)  10.6 us
    all_to_all x1, blocking collectives, body(): lax.all_to_all(fields, 'slab', split_axis=2, concat_axis=1, tiled=True)  10.3 us
    ppermute x3, starting transfers between devices, body(): lax.ppermute(going_down, 'col', [(d, (d - 1) % ways) for d in range(ways)])  9.45 us
    convert_element_type x1, other arithmetic, body(): gram = lax.psum_scatter(terms.astype(jnp.bfloat16), 'slab', scatter_dimen...  6.65 us
    another operation x1, other arithmetic, pair_terms(): return jnp.stack([real, imag])  6.35 us
    dot_general x1, matrix products, pair_terms(): lax.dot_general(left_imag, right_imag, dims, preferred_element_type=jnp.f...  6.12 us
  transfers between devices with their start and end apart: 9, of which 6 were waited for; matrix products, arithmetic and copies ran while one was open for 1% of the time, Pallas kernels for 0%

profile of v1, /device:TPU:1, one launch (start us, length us, event | category | flops | bytes accessed | tf_op | source)
XLA Modules:
  0.0 201.4 jit_solution(10168267526684357244)
XLA Ops:
  6.5 1.3 copy.3
  7.8 0.4 reshape
  8.2 10.3 %all_to_all.18 = bf16[2,2,32768]{2,1,0:T(2,128)(2,1)S(1)} all-to-all(bf16[2,2,32768]{2,1,0:T(2,128)(2,1)S(1)} %reshape), channel_id=1, replica_groups=mesh['row'=16,'col'=8,'slab'=2] {'slab'}, dimensions={0} | all-to-all | bytes 524288 | tf_op jit(solution)/shard_map/all_to_all | solution.py:17
  18.6 0.3 reshape.1
  18.9 1.0 copy.5
  20.0 0.0 reduce-scatter.2.cloned.1.call-start
  20.0 1.7 collective-permute-start
  21.7 4.0 %collective-permute-start.1 = (bf16[2,128,512]{2,1,0:T(8,128)(2,1)}, bf16[2,128,512]{2,1,0:T(8,128)(2,1)S(1)}, u32[]{:S(2)}, u32[]{:S(2)}) collective-permute-start(bf16[2,128,512]{2,1,0:T(8,128)(2,1)} %bitcast.23), channel_id=1, source_target_pairs={{0,14},{2,0},{4,2},{6,4},{8,6},{10,8},{12,10},{14,12},{1,15},{3,1}... | collective-permute-start | bytes 786440 | tf_op jit(solution)/shard_map/ppermute | solution.py:30
  25.8 4.6 %collective-permute-done = bf16[2,128,512]{2,1,0:T(8,128)(2,1)S(1)} collective-permute-done((bf16[2,128,512]{2,1,0:T(8,128)(2,1)}, bf16[2,128,512]{2,1,0:T(8,128)(2,1)S(1)}, u32[]{:S(2)}, u32[]{:S(2)}) %collective-permute-start) | collective-permute-done | bytes 262176 | tf_op jit(solution)/shard_map/ppermute | solution.py:25
  30.4 2.7 %collective-permute-start.3 = (bf16[2,128,512]{2,1,0:T(8,128)(2,1)S(1)}, bf16[2,128,512]{2,1,0:T(8,128)(2,1)S(1)}, u32[]{:S(2)}, u32[]{:S(2)}) collective-permute-start(bf16[2,128,512]{2,1,0:T(8,128)(2,1)S(1)} %collective-permute-done.1), channel_id=1, source_target_pairs={{0,14},{2,0},{4,2},{6,4},{8,6},{10,8},{12,10},{14,12},{1,15},{3,1}... | collective-permute-start | bytes 786440 | tf_op jit(solution)/shard_map/ppermute | solution.py:30
  33.1 0.1 broadcast_in_dim.3
  33.3 3.6 %collective-permute-done.2 = bf16[2,128,512]{2,1,0:T(8,128)(2,1)S(1)} collective-permute-done((bf16[2,128,512]{2,1,0:T(8,128)(2,1)S(1)}, bf16[2,128,512]{2,1,0:T(8,128)(2,1)S(1)}, u32[]{:S(2)}, u32[]{:S(2)}) %collective-permute-start.2) | collective-permute-done | bytes 262176 | tf_op jit(solution)/shard_map/ppermute | solution.py:25
  36.9 2.7 %collective-permute-start.5 = (bf16[2,128,512]{2,1,0:T(8,128)(2,1)S(1)}, bf16[2,128,512]{2,1,0:T(8,128)(2,1)S(1)}, u32[]{:S(2)}, u32[]{:S(2)}) collective-permute-start(bf16[2,128,512]{2,1,0:T(8,128)(2,1)S(1)} %collective-permute-done.3), channel_id=1, source_target_pairs={{0,14},{2,0},{4,2},{6,4},{8,6},{10,8},{12,10},{14,12},{1,15},{3,1}... | collective-permute-start | bytes 786440 | tf_op jit(solution)/shard_map/ppermute | solution.py:30
  39.7 3.6 %collective-permute-done.4 = bf16[2,128,512]{2,1,0:T(8,128)(2,1)S(1)} collective-permute-done((bf16[2,128,512]{2,1,0:T(8,128)(2,1)S(1)}, bf16[2,128,512]{2,1,0:T(8,128)(2,1)S(1)}, u32[]{:S(2)}, u32[]{:S(2)}) %collective-permute-start.4) | collective-permute-done | bytes 262176 | tf_op jit(solution)/shard_map/ppermute | solution.py:25
  43.4 7.1 %collective-permute-done.6 = bf16[2,128,512]{2,1,0:T(8,128)(2,1)S(1)} collective-permute-done((bf16[2,128,512]{2,1,0:T(8,128)(2,1)S(1)}, bf16[2,128,512]{2,1,0:T(8,128)(2,1)S(1)}, u32[]{:S(2)}, u32[]{:S(2)}) %collective-permute-start.6) | collective-permute-done | bytes 262176 | tf_op jit(solution)/shard_map/ppermute | solution.py:25
  50.5 0.1 fusion.16
  50.5 1.1 slice_bitcast_fusion.2
  51.6 10.6 %all-gather.2.cloned.1.call-done = bf16[2,2048,512]{2,1,0:T(8,128)(2,1)} async-done(((bf16[2,128,512]{2,1,0:T(8,128)(2,1)}), bf16[2,2048,512]{2,1,0:T(8,128)(2,1)}) %all-gather.2.cloned.1.call-update) | async-done | bytes 4194320 | tf_op jit(solution)/shard_map/all_gather | solution.py:36
  62.3 2.6 %slice_bitcast_fusion = (bf16[2048,512]{1,0:T(8,128)(2,1)S(1)}, bf16[2048,512]{1,0:T(8,128)(2,1)S(1)}) fusion(bf16[2,2048,512]{2,1,0:T(8,128)(2,1)} %all-gather.2.cloned.1.call-done), kind=kLoop, calls=%fused_computation.13 | loop fusion | bytes 8388608 | tf_op jit(solution)/shard_map/squeeze | solution.py:8
  64.9 4.8 %convert_bitcast_fusion.1 = bf16[1,1024,2048]{2,1,0:T(8,128)(2,1)S(1)} fusion(bf16[2048,512]{1,0:T(8,128)(2,1)S(1)} %get-tuple-element.5, bf16[2048,512]{1,0:T(8,128)(2,1)S(1)} %get-tuple-element.6, bf16[1024,512]{1,0:T(8,128)(2,1)S(1)} %get-tuple-element.8, bf16[1024,512]{1,0:T(8,128)(2,1)S(1)} %copy-done.1), kind=kOutput, calls=%fused_computation.10 | convolution fusion | flops 4309647360 | bytes 10485760 | tf_op jit(solution)/shard_map/dot_general | solution.py:11
  69.7 6.1 %convert_bitcast_fusion = bf16[1,1024,2048]{2,1,0:T(8,128)(2,1)} fusion(bf16[2048,512]{1,0:T(8,128)(2,1)S(1)} %get-tuple-element.6, bf16[2048,512]{1,0:T(8,128)(2,1)S(1)} %get-tuple-element.5, bf16[1024,512]{1,0:T(8,128)(2,1)S(1)} %get-tuple-element.8, bf16[1024,512]{1,0:T(8,128)(2,1)S(1)} %fusion.16), kind=kOutput, calls=%fused_computation.9 | convolution fusion | flops 4309647360 | bytes 10485760 | tf_op jit(solution)/shard_map/dot_general | solution.py:12
  75.8 6.3 %pad_maximum_fusion = bf16[2,1024,2048]{2,1,0:T(8,128)(2,1)} fusion(bf16[1,1024,2048]{2,1,0:T(8,128)(2,1)} %convert_bitcast_fusion, bf16[1,1024,2048]{2,1,0:T(8,128)(2,1)S(1)} %convert_bitcast_fusion.1), kind=kLoop, calls=%fused_computation | loop fusion | flops 4194304 | bytes 16777216 | tf_op jit(solution)/shard_map/stack | solution.py:13
  82.1 105.8 %reduce-scatter.2.cloned.1.call-done = bf16[2,512,2048]{2,1,0:T(8,128)(2,1)} async-done(((bf16[2,1024,2048]{2,1,0:T(8,128)(2,1)}), bf16[2,512,2048]{2,1,0:T(8,128)(2,1)}) %reduce-scatter.2.cloned.1.call-update) | async-done | bytes 4194320 | tf_op jit(solution)/shard_map/reduce_scatter | solution.py:38
  187.9 6.7 %convert_element_type.4 = f32[2,512,2048]{2,1,0:T(8,128)} convert(bf16[2,512,2048]{2,1,0:T(8,128)(2,1)} %reduce-scatter.2.cloned.1.call-done) | non-fusion elementwise | flops 2097152 | bytes 12582912 | tf_op jit(solution)/shard_map/convert_element_type | solution.py:40
  (21 shorter events, 0.2 us)
Async XLA Ops:
  6.5 55.7 %all-gather.2.cloned.1.call-start = ((), (), s32[]{:S(2)}) async-start(), calls=%async_computation.2 | async-start | bytes 4456448 | tf_op jit(solution)/shard_map/all_gather | solution.py:36
  20.0 13.3 %copy-start = (bf16[2,2,64,512]{3,2,1,0:T(8,128)(2,1)S(1)}, bf16[2,2,64,512]{3,2,1,0:T(8,128)(2,1)}, u32[]{:S(2)}) copy-start(bf16[2,2,64,512]{3,2,1,0:T(8,128)(2,1)} %copy.5) | copy-start | bytes 786436
  20.0 167.9 %reduce-scatter.2.cloned.1.call-start = ((), (), s32[]{:S(2)}) async-start(), calls=%async_computation.3 | async-start | bytes 12582912 | tf_op jit(solution)/shard_map/reduce_scatter | solution.py:38
  20.0 10.4 %collective-permute-start = (bf16[2,128,512]{2,1,0:T(8,128)(2,1)}, bf16[2,128,512]{2,1,0:T(8,128)(2,1)S(1)}, u32[]{:S(2)}, u32[]{:S(2)}) collective-permute-start(bf16[2,128,512]{2,1,0:T(8,128)(2,1)} %bitcast.22), channel_id=1, source_target_pairs={{0,2},{2,4},{4,6},{6,8},{8,10},{10,12},{12,14},{14,0},{1,3},{3,5},... | collective-permute-start | bytes 786440 | tf_op jit(solution)/shard_map/ppermute | solution.py:25
  21.7 8.7 %collective-permute-start.1 = (bf16[2,128,512]{2,1,0:T(8,128)(2,1)}, bf16[2,128,512]{2,1,0:T(8,128)(2,1)S(1)}, u32[]{:S(2)}, u32[]{:S(2)}) collective-permute-start(bf16[2,128,512]{2,1,0:T(8,128)(2,1)} %bitcast.23), channel_id=1, source_target_pairs={{0,14},{2,0},{4,2},{6,4},{8,6},{10,8},{12,10},{14,12},{1,15},{3,1}... | collective-permute-start | bytes 786440 | tf_op jit(solution)/shard_map/ppermute | solution.py:30
  30.4 6.4 %collective-permute-start.2 = (bf16[2,128,512]{2,1,0:T(8,128)(2,1)S(1)}, bf16[2,128,512]{2,1,0:T(8,128)(2,1)S(1)}, u32[]{:S(2)}, u32[]{:S(2)}) collective-permute-start(bf16[2,128,512]{2,1,0:T(8,128)(2,1)S(1)} %collective-permute-done), channel_id=1, source_target_pairs={{0,2},{2,4},{4,6},{6,8},{8,10},{10,12},{12,14},{14,0},{1,3},{3,5},... | collective-permute-start | bytes 786440 | tf_op jit(solution)/shard_map/ppermute | solution.py:25
  30.4 6.5 %collective-permute-start.3 = (bf16[2,128,512]{2,1,0:T(8,128)(2,1)S(1)}, bf16[2,128,512]{2,1,0:T(8,128)(2,1)S(1)}, u32[]{:S(2)}, u32[]{:S(2)}) collective-permute-start(bf16[2,128,512]{2,1,0:T(8,128)(2,1)S(1)} %collective-permute-done.1), channel_id=1, source_target_pairs={{0,14},{2,0},{4,2},{6,4},{8,6},{10,8},{12,10},{14,12},{1,15},{3,1}... | collective-permute-start | bytes 786440 | tf_op jit(solution)/shard_map/ppermute | solution.py:30
  36.8 6.4 %collective-permute-start.4 = (bf16[2,128,512]{2,1,0:T(8,128)(2,1)S(1)}, bf16[2,128,512]{2,1,0:T(8,128)(2,1)S(1)}, u32[]{:S(2)}, u32[]{:S(2)}) collective-permute-start(bf16[2,128,512]{2,1,0:T(8,128)(2,1)S(1)} %collective-permute-done.2), channel_id=1, source_target_pairs={{0,2},{2,4},{4,6},{6,8},{8,10},{10,12},{12,14},{14,0},{1,3},{3,5},... | collective-permute-start | bytes 786440 | tf_op jit(solution)/shard_map/ppermute | solution.py:25
  36.9 6.4 %collective-permute-start.5 = (bf16[2,128,512]{2,1,0:T(8,128)(2,1)S(1)}, bf16[2,128,512]{2,1,0:T(8,128)(2,1)S(1)}, u32[]{:S(2)}, u32[]{:S(2)}) collective-permute-start(bf16[2,128,512]{2,1,0:T(8,128)(2,1)S(1)} %collective-permute-done.3), channel_id=1, source_target_pairs={{0,14},{2,0},{4,2},{6,4},{8,6},{10,8},{12,10},{14,12},{1,15},{3,1}... | collective-permute-start | bytes 786440 | tf_op jit(solution)/shard_map/ppermute | solution.py:30
  43.3 7.2 %collective-permute-start.6 = (bf16[2,128,512]{2,1,0:T(8,128)(2,1)S(1)}, bf16[2,128,512]{2,1,0:T(8,128)(2,1)S(1)}, u32[]{:S(2)}, u32[]{:S(2)}) collective-permute-start(bf16[2,128,512]{2,1,0:T(8,128)(2,1)S(1)} %collective-permute-done.4), channel_id=1, source_target_pairs={{0,2},{2,4},{4,6},{6,8},{8,10},{10,12},{12,14},{14,0},{1,3},{3,5},... | collective-permute-start | bytes 786440 | tf_op jit(solution)/shard_map/ppermute | solution.py:25
  62.3 2.6 %copy-start.1 = (bf16[1024,512]{1,0:T(8,128)(2,1)S(1)}, bf16[1024,512]{1,0:T(8,128)(2,1)}, u32[]{:S(2)}) copy-start(bf16[1024,512]{1,0:T(8,128)(2,1)} %get-tuple-element.7) | copy-start | bytes 3145732
Sparse Core Ops, SparseCore 0:
  20.1 42.1 all-gather.1
  82.3 105.5 reduce-scatter.1
